TPU v7x, 32 devices: a whole 2x2x4 slice. The times are simulated.
32 devices in a mesh: groups: 2 (over y), space: 4 (over z), disp: 4 (over x, core).
Axes of the slice: x: 2, y: 2, z: 4, core: 2. Of those that a mesh axis runs over, the one named last changes fastest.
Arguments:
- volume: bfloat16 [8, 16, 32, 256], P(None, 'disp', ('groups', 'space')), parts along dimension 2, may hold values from -6 to 6
- w_first: bfloat16 [3, 3, 3, 8, 8], replicated, may hold values from -0.4375 to 0.4375
- b_first: float32 [8], replicated, may hold values from -1 to 1
- w_second: bfloat16 [3, 3, 3, 8], replicated, may hold values from -0.4375 to 0.4375
- prior_logits: float32 [16, 32, 256], P('disp', ('groups', 'space')), parts along dimension 1, may hold values from -15 to 310
- cotangent: float32 [32, 256], P(('groups', 'space')), parts along dimension 0, may hold values from -24 to 24
Outputs:
- grad_volume: bfloat16 [8, 16, 32, 256], P(None, 'disp', ('groups', 'space')), parts along dimension 2
- grad_w_first: float32 [3, 3, 3, 16, 8], P(None, None, None, 'groups'), parts along dimension 3
- grad_b_first: float32 [16], P('groups'), parts along dimension 0
- grad_w_second: float32 [3, 3, 3, 16], P(None, None, None, 'groups'), parts along dimension 3
- disparity: float32 [32, 256], P(('groups', 'space')), parts along dimension 0
There are 2 independent parts, one for each index of `groups`. A program takes and returns all parts, laid end to end along the dimension named above; an argument that names none is the same for every part. Nothing has to cross between parts.
All inputs are finite; a program needn't handle non-finite values.
Results may differ from a plain program's by a relative error of at most 0.011.
Values may be sent and summed in bfloat16 or wider, within the bound.
No kernel may reach another device: no remote copies, remote signals or barrier semaphores. Data moves between devices by JAX's collectives and lax.ppermute only.
A program may use at most 64 MiB of HBM per device.

v0:
```python
import math
import jax
import jax.numpy as jnp
from jax import lax
from jax.sharding import PartitionSpec as P


def padded_2(cells, sides, width):
    for axis, dim in sides:
        count = lax.axis_size(axis)
        ends = count - 1
        head = lax.slice_in_dim(cells, 0, width, axis=dim)
        tail = lax.slice_in_dim(cells, cells.shape[dim] - width, cells.shape[dim], axis=dim)
        cells = jnp.concatenate(
            [
                lax.ppermute(tail, axis, [(i, (i + 1) % count) for i in range(ends)]),
                cells,
                lax.ppermute(head, axis, [((i + 1) % count, i) for i in range(ends)]),
            ],
            axis=dim,
        )
    return cells


def combined_all(value, axis, combine):
    everything = jax.tree.map(lambda part: lax.all_gather(part, axis), value)
    first = jax.tree.map(lambda part: part[0], everything)

    def step(k, so_far):
        return combine(so_far, jax.tree.map(lambda part: part[k], everything))

    return lax.fori_loop(1, lax.axis_size(axis), step, first)


def tap_stack(source, planes, rows, width):
    padded = jnp.pad(source, ((0, 0), (0, 0), (0, 0), (1, 1)))
    return jnp.concatenate(
        [
            padded[:, a : a + planes, b : b + rows, c : c + width]
            for a in range(3)
            for b in range(3)
            for c in range(3)
        ],
        axis=0,
    )


def correlate(source, kernel):
    planes = source.shape[1] - 2
    rows = source.shape[2] - 2
    width = source.shape[3]
    stacked = tap_stack(source, planes, rows, width)
    joined = jnp.concatenate(
        [kernel[a, b, c] for a in range(3) for b in range(3) for c in range(3)], axis=1
    )
    return jnp.einsum("oi,idhw->odhw", joined, stacked, preferred_element_type=jnp.float32)


def transposed(kernel):
    return jnp.swapaxes(kernel[::-1, ::-1, ::-1], 3, 4)


def kernel_grad(out_grad, source):
    planes = out_grad.shape[1]
    rows = out_grad.shape[2]
    width = out_grad.shape[3]
    stacked = tap_stack(source, planes, rows, width)
    product = jnp.einsum("odhw,kdhw->ok", out_grad, stacked, preferred_element_type=jnp.float32)
    outputs = product.shape[0]
    inputs = source.shape[0]
    return jnp.transpose(product.reshape(outputs, 3, 3, 3, inputs), (1, 2, 3, 0, 4))


def inside_mask(planes, rows, reach, plane_count, row_count):
    plane_index = (
        lax.axis_index("disp") * plane_count
        - reach
        + lax.broadcasted_iota(jnp.int32, (planes, rows, 1), 0)
    )
    row_index = (
        lax.axis_index("space") * row_count
        - reach
        + lax.broadcasted_iota(jnp.int32, (planes, rows, 1), 1)
    )
    keeper = (
        (plane_index >= 0)
        & (plane_index < plane_count * lax.axis_size("disp"))
        & (row_index >= 0)
        & (row_index < row_count * lax.axis_size("space"))
    )
    return keeper.astype(jnp.float32)


def combine_stats(first_part, second_part):
    highest = jnp.maximum(first_part[0], second_part[0])
    factor_one = jnp.exp(first_part[0] - highest)
    factor_two = jnp.exp(second_part[0] - highest)
    return (
        highest,
        first_part[1] * factor_one + second_part[1] * factor_two,
        first_part[2] * factor_one + second_part[2] * factor_two,
    )


def silu_grad(hidden_grad, pre_act):
    gate_sigmoid = jax.nn.sigmoid(pre_act)
    return (hidden_grad * gate_sigmoid * (1.0 + pre_act * (1.0 - gate_sigmoid))).astype(
        jnp.bfloat16
    )


def shards(volume, w_first, b_first, w_second, prior_logits, cotangent):
    plane_count = volume.shape[1]
    row_count = volume.shape[2]
    width = volume.shape[3]
    disp_size = lax.axis_size("disp")
    space_size = lax.axis_size("space")
    extended = padded_2(volume, (("space", 2), ("disp", 1)), 2)
    pre_act = correlate(extended, w_first) + b_first[:, None, None, None]
    inside = inside_mask(plane_count + 2, row_count + 2, 1, plane_count, row_count)
    hidden = (jax.nn.silu(pre_act) * inside[None]).astype(jnp.bfloat16)
    second_kernel = w_second[:, :, :, None, :]
    logits = correlate(hidden, second_kernel)[0] + prior_logits
    plane_total = plane_count * disp_size
    position = (
        lax.axis_index("disp") * plane_count
        + lax.broadcasted_iota(jnp.int32, (plane_count, 1, 1), 0)
    ).astype(jnp.float32)
    position = (position + 0.5) / plane_total
    local_top = jnp.max(logits, axis=0)
    local_exp = jnp.exp(logits - local_top[None])
    highest, summed, moment = combined_all(
        (local_top, jnp.sum(local_exp, axis=0), jnp.sum(local_exp * position, axis=0)),
        "disp",
        combine_stats,
    )
    disparity = moment / summed
    probability = jnp.exp(logits - highest[None]) / summed[None]
    score_grad = (cotangent[None] * probability * (position - disparity[None])).astype(jnp.bfloat16)
    second_grad = kernel_grad(score_grad[None], hidden)[:, :, :, 0, :]
    flipped_second = transposed(second_kernel)
    score_border = padded_2(score_grad, (("space", 1), ("disp", 0)), 2)
    hidden_grad = correlate(score_border[None], flipped_second)
    grad_border = silu_grad(hidden_grad, pre_act) * inside[None].astype(jnp.bfloat16)
    pre_grad = grad_border[:, 1:-1, 1:-1]
    volume_grad = correlate(grad_border, transposed(w_first)).astype(jnp.bfloat16)
    first_grad = kernel_grad(pre_grad, extended[:, 1:-1, 1:-1])
    bias_grad = jnp.sum(pre_grad, axis=(1, 2, 3), dtype=jnp.float32)
    grad_scale = 16.0 / math.sqrt(plane_total * row_count * space_size * width)
    first_sum, bias_sum, second_sum = lax.psum(
        (first_grad * grad_scale, bias_grad * grad_scale, second_grad * grad_scale),
        ("space", "disp"),
    )
    return (volume_grad, first_sum, bias_sum, second_sum, disparity)


def solution(mesh):
    return jax.shard_map(
        shards,
        mesh=mesh,
        in_specs=(
            P(None, "disp", ("groups", "space"), None),
            P(),
            P(),
            P(),
            P("disp", ("groups", "space"), None),
            P(("groups", "space"), None),
        ),
        out_specs=(
            P(None, "disp", ("groups", "space"), None),
            P(None, None, None, "groups", None),
            P("groups"),
            P(None, None, None, "groups"),
            P(("groups", "space"), None),
        ),
        check_vma=False,
    )
```

profile of v0, /device:TPU:0, one launch (start us, length us, event | category | flops | bytes accessed | tf_op | source)
XLA Modules:
  0.0 138.1 jit_solution(7539240962752502792)
XLA Ops:
  0.6 0.9 copy.121
  1.5 4.9 %collective-permute-start = (bf16[8,4,2,256]{3,0,2,1:T(8,128)(2,1)S(1)}, bf16[8,4,2,256]{3,0,2,1:T(8,128)(2,1)S(1)}, u32[]{:S(2)}, u32[]{:S(2)}) collective-permute-start(bf16[8,4,2,256]{3,0,2,1:T(8,128)(2,1)S(1)} %get-tuple-element.256), channel_id=1, source_target_pairs={{0,4},{4,8},{8,12},{1,5},{5,9},{9,13},{2,6},{6,10},{10,14},{3,7},{... | collective-permute-start | bytes 98312 | tf_op jit(solution)/shard_map/ppermute | solution.py:16
  6.5 1.3 collective-permute-start.1
  7.8 0.9 slice_bitcast_fusion.30
  8.6 0.8 slice_bitcast_fusion.31
  9.4 0.9 slice_bitcast_fusion.57
  10.3 0.8 slice_bitcast_fusion.76
  11.1 0.7 reverse.3
  11.9 0.9 copy.93
  13.0 0.1 copy.102
  13.1 0.1 copy.103
  13.2 0.1 copy.104
  15.6 0.1 concatenate.65
  15.7 0.1 concatenate.64
  15.8 0.1 concatenate.63
  15.9 0.1 concatenate.62
  16.1 0.9 constant_dynamic-update-slice_fusion.1
  17.0 1.5 %collective-permute-start.2 = (bf16[8,2,8,256]{3,0,2,1:T(8,128)(2,1)S(1)}, bf16[8,2,8,256]{3,0,2,1:T(8,128)(2,1)S(1)}, u32[]{:S(2)}, u32[]{:S(2)}) collective-permute-start(bf16[8,2,8,256]{3,0,2,1:T(8,128)(2,1)S(1)} %get-tuple-element.226), channel_id=1, source_target_pairs={{0,1},{1,2},{2,3},{4,5},{5,6},{6,7},{8,9},{9,10},{10,11},{12,13},{... | collective-permute-start | bytes 196616 | tf_op jit(solution)/shard_map/ppermute | solution.py:16
  18.5 1.3 collective-permute-start.3
  19.8 3.4 %collective-permute-done.3 = bf16[8,2,8,256]{3,0,2,1:T(8,128)(2,1)S(1)} collective-permute-done((bf16[8,2,8,256]{3,0,2,1:T(8,128)(2,1)S(1)}, bf16[8,2,8,256]{3,0,2,1:T(8,128)(2,1)S(1)}, u32[]{:S(2)}, u32[]{:S(2)}) %collective-permute-start.3) | collective-permute-done | bytes 65568 | tf_op jit(solution)/shard_map/ppermute | solution.py:18
  23.2 0.1 constant_dynamic-update-slice_fusion.29
  23.3 0.1 constant_dynamic-update-slice_fusion.27
  23.4 0.1 constant_dynamic-update-slice_fusion.26
  23.6 0.1 constant_dynamic-update-slice_fusion.24
  23.7 0.1 constant_dynamic-update-slice_fusion.23
  23.8 0.1 constant_dynamic-update-slice_fusion.21
  23.9 0.1 constant_dynamic-update-slice_fusion.20
  24.1 0.1 constant_dynamic-update-slice_fusion.18
  24.2 0.1 constant_dynamic-update-slice_fusion.17
  24.3 0.1 constant_dynamic-update-slice_fusion.15
  24.5 0.1 constant_dynamic-update-slice_fusion.14
  24.6 0.1 constant_dynamic-update-slice_fusion.12
  24.7 0.1 constant_dynamic-update-slice_fusion.11
  24.8 0.1 constant_dynamic-update-slice_fusion.9
  25.0 0.1 constant_dynamic-update-slice_fusion.8
  25.1 0.1 constant_dynamic-update-slice_fusion.6
  25.2 0.1 constant_dynamic-update-slice_fusion.5
  25.4 0.1 constant_dynamic-update-slice_fusion.3
  25.5 0.7 multiply_convert_fusion
  28.0 0.4 fusion.24
  28.5 6.8 %all-gather.5 = f32[4,4,256]{2,1,0:T(4,128)S(1)} all-gather(f32[1,4,256]{2,1,0:T(4,128)S(1)} %bitcast.306), channel_id=4, replica_groups=mesh['groups'=2,'space'=4,'disp'=4] {'disp'}, dimensions={0}, use_global_device_ids=true | all-gather | bytes 20480 | tf_op jit(solution)/shard_map/all_gather | solution.py:26
  35.2 5.2 %all-gather.4 = f32[4,4,256]{2,1,0:T(4,128)S(1)} all-gather(f32[1,4,256]{2,1,0:T(4,128)S(1)} %bitcast.305), channel_id=3, replica_groups=mesh['groups'=2,'space'=4,'disp'=4] {'disp'}, dimensions={0}, use_global_device_ids=true | all-gather | bytes 20480 | tf_op jit(solution)/shard_map/all_gather | solution.py:26
  40.4 5.2 %all-gather.3 = f32[4,4,256]{2,1,0:T(4,128)S(1)} all-gather(f32[1,4,256]{2,1,0:T(4,128)S(1)} %bitcast.304), channel_id=2, replica_groups=mesh['groups'=2,'space'=4,'disp'=4] {'disp'}, dimensions={0}, use_global_device_ids=true | all-gather | bytes 20480 | tf_op jit(solution)/shard_map/all_gather | solution.py:26
  45.6 0.2 while.19
  46.0 3.9 %fusion.3 = f32[1,3,3,3,8,1,1]{4,0,6,5,3,2,1:T(1,128)S(1)} fusion(bf16[3,3,3,8,4,4,256]{6,3,2,1,0,5,4:T(8,128)(2,1)S(1)} %bitcast.298, bf16[4,4,256,1,1,1,1]{2,1,0,3,4,5,6:T(4,128)(2,1)S(1)} %fusion.42), kind=kOutput, calls=%fused_computation.8 | convolution fusion | flops 1769472 | bytes 1778528 | tf_op jit(solution)/shard_map/odhw,kdhw->ok/dot_general | solution.py:68
  51.6 4.5 %collective-permute-start.4 = (bf16[4,2,256]{2,1,0:T(2,128)(2,1)S(1)}, bf16[4,2,256]{2,1,0:T(2,128)(2,1)S(1)}, u32[]{:S(2)}, u32[]{:S(2)}) collective-permute-start(bf16[4,2,256]{2,1,0:T(2,128)(2,1)S(1)} %get-tuple-element.367), channel_id=1, source_target_pairs={{0,4},{4,8},{8,12},{1,5},{5,9},{9,13},{2,6},{6,10},{10,14},{3,7},{... | collective-permute-start | bytes 12296 | tf_op jit(solution)/shard_map/ppermute | solution.py:16
  56.2 1.3 collective-permute-start.5
  57.5 4.2 %collective-permute-done.5 = bf16[4,2,256]{2,1,0:T(2,128)(2,1)S(1)} collective-permute-done((bf16[4,2,256]{2,1,0:T(2,128)(2,1)S(1)}, bf16[4,2,256]{2,1,0:T(2,128)(2,1)S(1)}, u32[]{:S(2)}, u32[]{:S(2)}) %collective-permute-start.5) | collective-permute-done | bytes 4128 | tf_op jit(solution)/shard_map/ppermute | solution.py:18
  61.7 1.3 collective-permute-start.6
  63.0 1.3 collective-permute-start.7
  64.4 3.2 %collective-permute-done.7 = bf16[2,8,256]{2,1,0:T(8,128)(2,1)S(1)} collective-permute-done((bf16[2,8,256]{2,1,0:T(8,128)(2,1)S(1)}, bf16[2,8,256]{2,1,0:T(8,128)(2,1)S(1)}, u32[]{:S(2)}, u32[]{:S(2)}) %collective-permute-start.7) | collective-permute-done | bytes 8224 | tf_op jit(solution)/shard_map/ppermute | solution.py:18
  67.7 0.6 pad_slice_fusion.93
  68.3 0.6 pad_slice_fusion.92
  68.9 0.2 fusion.32
  69.2 1.7 %concatenate.74 = bf16[27,6,6,256]{3,0,2,1:T(8,128)(2,1)S(1)} concatenate(bf16[1,6,6,256]{3,0,2,1:T(2,128)(2,1)S(1)} %get-tuple-element.254, bf16[1,6,6,256]{3,0,2,1:T(2,128)(2,1)S(1)} %get-tuple-element.253, bf16[1,6,6,256]{3,0,2,1:T(2,128)(2,1)S(1)} %get-tuple-element.229, bf16[1,6,6,256]{3,0,2,1:T(2,128)(2,1)S(1)} %get-tuple-element.230, ...), dimensions={0} | concatenate | bytes 995328 | tf_op jit(solution)/shard_map/concatenate | solution.py:37
  70.9 0.2 fusion.7
  71.1 0.1 convert_reduce_fusion
  71.4 1.0 copy-done.1
  72.4 0.6 fusion.8
  72.9 0.1 mul.133
  73.1 61.6 %all-reduce.5 = (f32[3,3,3,8,8]{4,2,1,0,3:T(4,128)S(1)}, f32[8]{0:T(128)}, f32[3,3,3,8]{3,2,1,0:T(4,128)}) all-reduce(f32[3,3,3,8,8]{4,2,1,0,3:T(4,128)S(1)} %bitcast.299, f32[8]{0:T(128)S(1)} %broadcast_multiply_fusion, f32[3,3,3,8]{3,2,1,0:T(4,128)S(1)} %bitcast_multiply_fusion.2), channel_id=1, replica_groups=mesh['groups'=2,'space'=4,'disp'=4] {'space','disp'}, use_global_device_ids=true, to_apply=%region_5.6 | all-reduce | flops 1952 | bytes 15616 | tf_op jit(solution)/shard_map/psum | solution.py:150
  134.7 0.7 copy.138
  137.1 0.4 convolution_convert_fusion
  137.4 0.7 copy.137
  (170 shorter events, 8.0 us)
Async XLA Ops:
  1.5 14.5 %collective-permute-start = (bf16[8,4,2,256]{3,0,2,1:T(8,128)(2,1)S(1)}, bf16[8,4,2,256]{3,0,2,1:T(8,128)(2,1)S(1)}, u32[]{:S(2)}, u32[]{:S(2)}) collective-permute-start(bf16[8,4,2,256]{3,0,2,1:T(8,128)(2,1)S(1)} %get-tuple-element.256), channel_id=1, source_target_pairs={{0,4},{4,8},{8,12},{1,5},{5,9},{9,13},{2,6},{6,10},{10,14},{3,7},{... | collective-permute-start | bytes 98312 | tf_op jit(solution)/shard_map/ppermute | solution.py:16
  6.5 10.5 %collective-permute-start.1 = (bf16[8,4,2,256]{3,0,2,1:T(8,128)(2,1)S(1)}, bf16[8,4,2,256]{3,0,2,1:T(8,128)(2,1)S(1)}, u32[]{:S(2)}, u32[]{:S(2)}) collective-permute-start(bf16[8,4,2,256]{3,0,2,1:T(8,128)(2,1)S(1)} %get-tuple-element.255), channel_id=1, source_target_pairs={{4,0},{8,4},{12,8},{5,1},{9,5},{13,9},{6,2},{10,6},{14,10},{7,3},{... | collective-permute-start | bytes 98312 | tf_op jit(solution)/shard_map/ppermute | solution.py:18
  17.0 2.8 %collective-permute-start.2 = (bf16[8,2,8,256]{3,0,2,1:T(8,128)(2,1)S(1)}, bf16[8,2,8,256]{3,0,2,1:T(8,128)(2,1)S(1)}, u32[]{:S(2)}, u32[]{:S(2)}) collective-permute-start(bf16[8,2,8,256]{3,0,2,1:T(8,128)(2,1)S(1)} %get-tuple-element.226), channel_id=1, source_target_pairs={{0,1},{1,2},{2,3},{4,5},{5,6},{6,7},{8,9},{9,10},{10,11},{12,13},{... | collective-permute-start | bytes 196616 | tf_op jit(solution)/shard_map/ppermute | solution.py:16
  18.5 4.7 %collective-permute-start.3 = (bf16[8,2,8,256]{3,0,2,1:T(8,128)(2,1)S(1)}, bf16[8,2,8,256]{3,0,2,1:T(8,128)(2,1)S(1)}, u32[]{:S(2)}, u32[]{:S(2)}) collective-permute-start(bf16[8,2,8,256]{3,0,2,1:T(8,128)(2,1)S(1)} %get-tuple-element.227), channel_id=1, source_target_pairs={{1,0},{2,1},{3,2},{5,4},{6,5},{7,6},{9,8},{10,9},{11,10},{13,12},{... | collective-permute-start | bytes 196616 | tf_op jit(solution)/shard_map/ppermute | solution.py:18
  24.7 0.8 copy-start.6
  27.4 1.0 copy-start.4
  27.6 18.2 %copy-start.5 = (f32[4,256]{1,0:T(4,128)S(1)}, f32[4,256]{1,0:T(4,128)}, u32[]{:S(2)}) copy-start(f32[4,256]{1,0:T(4,128)} %param.13) | copy-start | bytes 12292
  45.8 4.4 %copy-start.3 = (f32[4,256]{1,0:T(4,128)}, f32[4,256]{1,0:T(4,128)S(1)}, u32[]{:S(2)}) copy-start(f32[4,256]{1,0:T(4,128)S(1)} %div.23) | copy-start | bytes 12292
  49.9 0.9 copy-start.2
  51.6 5.9 %collective-permute-start.4 = (bf16[4,2,256]{2,1,0:T(2,128)(2,1)S(1)}, bf16[4,2,256]{2,1,0:T(2,128)(2,1)S(1)}, u32[]{:S(2)}, u32[]{:S(2)}) collective-permute-start(bf16[4,2,256]{2,1,0:T(2,128)(2,1)S(1)} %get-tuple-element.367), channel_id=1, source_target_pairs={{0,4},{4,8},{8,12},{1,5},{5,9},{9,13},{2,6},{6,10},{10,14},{3,7},{... | collective-permute-start | bytes 12296 | tf_op jit(solution)/shard_map/ppermute | solution.py:16
  56.2 5.5 %collective-permute-start.5 = (bf16[4,2,256]{2,1,0:T(2,128)(2,1)S(1)}, bf16[4,2,256]{2,1,0:T(2,128)(2,1)S(1)}, u32[]{:S(2)}, u32[]{:S(2)}) collective-permute-start(bf16[4,2,256]{2,1,0:T(2,128)(2,1)S(1)} %get-tuple-element.368), channel_id=1, source_target_pairs={{4,0},{8,4},{12,8},{5,1},{9,5},{13,9},{6,2},{10,6},{14,10},{7,3},{... | collective-permute-start | bytes 12296 | tf_op jit(solution)/shard_map/ppermute | solution.py:18
  61.7 2.7 %collective-permute-start.6 = (bf16[2,8,256]{2,1,0:T(8,128)(2,1)S(1)}, bf16[2,8,256]{2,1,0:T(8,128)(2,1)S(1)}, u32[]{:S(2)}, u32[]{:S(2)}) collective-permute-start(bf16[2,8,256]{2,1,0:T(8,128)(2,1)S(1)} %get-tuple-element.311), channel_id=1, source_target_pairs={{0,1},{1,2},{2,3},{4,5},{5,6},{6,7},{8,9},{9,10},{10,11},{12,13},{... | collective-permute-start | bytes 24584 | tf_op jit(solution)/shard_map/ppermute | solution.py:16
  63.0 4.6 %collective-permute-start.7 = (bf16[2,8,256]{2,1,0:T(8,128)(2,1)S(1)}, bf16[2,8,256]{2,1,0:T(8,128)(2,1)S(1)}, u32[]{:S(2)}, u32[]{:S(2)}) collective-permute-start(bf16[2,8,256]{2,1,0:T(8,128)(2,1)S(1)} %get-tuple-element.312), channel_id=1, source_target_pairs={{1,0},{2,1},{3,2},{5,4},{6,5},{7,6},{9,8},{10,9},{11,10},{13,12},{... | collective-permute-start | bytes 24584 | tf_op jit(solution)/shard_map/ppermute | solution.py:18
  64.4 3.2 %copy-start = (bf16[216,4,4,256]{3,0,2,1:T(8,128)(2,1)}, bf16[216,4,4,256]{3,0,2,1:T(8,128)(2,1)S(1)}, u32[]{:S(2)}) copy-start(bf16[216,4,4,256]{3,0,2,1:T(8,128)(2,1)S(1)} %constant_dynamic-update-slice_fusion.84) | copy-start | bytes 5308420
  70.9 1.5 %copy-start.1 = (bf16[216,4,4,256]{3,0,2,1:T(8,128)(2,1)S(1)}, bf16[216,4,4,256]{3,0,2,1:T(8,128)(2,1)}, u32[]{:S(2)}) copy-start(bf16[216,4,4,256]{3,0,2,1:T(8,128)(2,1)} %copy-done) | copy-start | bytes 5308420
where the time goes:
time: 139 us; the launch traced here: 138 us
  blocking collectives  78.7 us (57%)
  local copies, waits for them, and re-layouts  22.4 us (16%)
  starting transfers between devices  17.4 us (13%)
  waiting for transfers between devices  10.8 us (8%)
  matrix products  6.02 us (4%)
  between operations  1.86 us (1%)
    psum x1, blocking collectives, shards(): lax.psum((first_grad * grad_scale, bias_grad * grad_scale, second_grad *...  61.6 us
    all_gather x3, blocking collectives, combined_all(): everything = jax.tree.map(lambda part: lax.all_gather(part, axis), value)  17.1 us
    ppermute x4, starting transfers between devices, padded_2(): lax.ppermute(tail, axis, [(i, (i + 1) % count) for i in range(ends)])  12.2 us
    unnamed x109, local copies, waits for them, and re-layouts  11.4 us
    ppermute x4, waiting for transfers between devices, padded_2(): lax.ppermute(head, axis, [((i + 1) % count, i) for i in range(ends)])  10.8 us
    squeeze x35, local copies, waits for them, and re-layouts, correlate(): kernel[a, b, c]  5.99 us
    ppermute x4, starting transfers between devices, padded_2(): lax.ppermute(head, axis, [((i + 1) % count, i) for i in range(ends)])  5.17 us
    dot_general x2, matrix products, kernel_grad(): jnp.einsum('odhw,kdhw->ok', out_grad, stacked, preferred_element_type=jnp...  4.42 us
  transfers between devices with their start and end apart: 8, of which 3 were waited for; matrix products, arithmetic and copies ran while one was open for 7% of the time, Pallas kernels for 0%

commit v1 on v0

--- a/solution.py
+++ b/solution.py
@@ -148,8 +148,10 @@
     bias_grad = jnp.sum(pre_grad, axis=(1, 2, 3), dtype=jnp.float32)
     grad_scale = 16.0 / math.sqrt(plane_total * row_count * space_size * width)
     first_sum, bias_sum, second_sum = lax.psum(
-        (first_grad * grad_scale, bias_grad * grad_scale, second_grad * grad_scale),
-        ("space", "disp"),
+        lax.psum(
+            (first_grad * grad_scale, bias_grad * grad_scale, second_grad * grad_scale), "disp"
+        ),
+        "space",
     )
     return (volume_grad, first_sum, bias_sum, second_sum, disparity)
 

time: 139 us -> 112 us (0.81)
  blocking collectives: 78.7 us -> 52.3 us
    psum x1, blocking collectives: 61.6 us -> 14.4 us  [shards(): lax.psum((first_grad * grad_scale, bias_grad * grad_scale, second_grad *...]
    psum x0 -> x1, blocking collectives: none -> 20.9 us  [shards(): lax.psum(lax.psum((first_grad * grad_scale, bias_grad * grad_scale, secon...]
  transfers between devices with their start and end apart: 8 -> 8, of which waited for: 3 -> 3; matrix products, arithmetic and copies ran while one was open for 7% -> 8% of each run, Pallas kernels for 0% -> 0%
where the time goes in v1:
time: 112 us
  blocking collectives  52.3 us (47%)
  local copies, waits for them, and re-layouts  22.4 us (20%)
  starting transfers between devices  17.4 us (16%)
  waiting for transfers between devices  10.8 us (10%)
  matrix products  6.02 us (5%)
  between operations  1.86 us (2%)
    psum x1, blocking collectives, shards(): lax.psum(lax.psum((first_grad * grad_scale, bias_grad * grad_scale, secon...  20.9 us
    all_gather x3, blocking collectives, combined_all(): everything = jax.tree.map(lambda part: lax.all_gather(part, axis), value)  17.1 us
    psum x1, blocking collectives, shards(): lax.psum((first_grad * grad_scale, bias_grad * grad_scale, second_grad *...  14.4 us
    ppermute x4, starting transfers between devices, padded_2(): lax.ppermute(tail, axis, [(i, (i + 1) % count) for i in range(ends)])  12.2 us
    unnamed x109, local copies, waits for them, and re-layouts  11.4 us
    ppermute x4, waiting for transfers between devices, padded_2(): lax.ppermute(head, axis, [((i + 1) % count, i) for i in range(ends)])  10.8 us
    squeeze x35, local copies, waits for them, and re-layouts, correlate(): kernel[a, b, c]  5.99 us
    ppermute x4, starting transfers between devices, padded_2(): lax.ppermute(head, axis, [((i + 1) % count, i) for i in range(ends)])  5.17 us
  transfers between devices with their start and end apart: 8, of which 3 were waited for; matrix products, arithmetic and copies ran while one was open for 8% of the time, Pallas kernels for 0%

profile of v1, /device:TPU:0, one launch (start us, length us, event | category | flops | bytes accessed | tf_op | source)
XLA Modules:
  0.0 111.7 jit_solution(2006294606921522611)
XLA Ops:
  0.6 0.9 copy.121
  1.5 4.9 %collective-permute-start = (bf16[8,4,2,256]{3,0,2,1:T(8,128)(2,1)S(1)}, bf16[8,4,2,256]{3,0,2,1:T(8,128)(2,1)S(1)}, u32[]{:S(2)}, u32[]{:S(2)}) collective-permute-start(bf16[8,4,2,256]{3,0,2,1:T(8,128)(2,1)S(1)} %get-tuple-element.259), channel_id=1, source_target_pairs={{0,4},{4,8},{8,12},{1,5},{5,9},{9,13},{2,6},{6,10},{10,14},{3,7},{... | collective-permute-start | bytes 98312 | tf_op jit(solution)/shard_map/ppermute | solution.py:16
  6.5 1.3 %collective-permute-start.1 = (bf16[8,4,2,256]{3,0,2,1:T(8,128)(2,1)S(1)}, bf16[8,4,2,256]{3,0,2,1:T(8,128)(2,1)S(1)}, u32[]{:S(2)}, u32[]{:S(2)}) collective-permute-start(bf16[8,4,2,256]{3,0,2,1:T(8,128)(2,1)S(1)} %get-tuple-element.258), channel_id=1, source_target_pairs={{4,0},{8,4},{12,8},{5,1},{9,5},{13,9},{6,2},{10,6},{14,10},{7,3},{... | collective-permute-start | bytes 98312 | tf_op jit(solution)/shard_map/ppermute | solution.py:18
  7.8 0.9 slice_bitcast_fusion.30
  8.6 0.8 slice_bitcast_fusion.31
  9.4 0.9 slice_bitcast_fusion.57
  10.3 0.8 slice_bitcast_fusion.76
  11.1 0.7 reverse.3
  11.9 0.9 copy.93
  13.0 0.1 copy.102
  13.1 0.1 copy.103
  15.6 0.1 concatenate.65
  15.7 0.1 concatenate.64
  15.8 0.1 concatenate.63
  15.9 0.1 concatenate.62
  16.1 0.9 constant_dynamic-update-slice_fusion.1
  17.0 1.5 %collective-permute-start.2 = (bf16[8,2,8,256]{3,0,2,1:T(8,128)(2,1)S(1)}, bf16[8,2,8,256]{3,0,2,1:T(8,128)(2,1)S(1)}, u32[]{:S(2)}, u32[]{:S(2)}) collective-permute-start(bf16[8,2,8,256]{3,0,2,1:T(8,128)(2,1)S(1)} %get-tuple-element.229), channel_id=1, source_target_pairs={{0,1},{1,2},{2,3},{4,5},{5,6},{6,7},{8,9},{9,10},{10,11},{12,13},{... | collective-permute-start | bytes 196616 | tf_op jit(solution)/shard_map/ppermute | solution.py:16
  18.5 1.3 %collective-permute-start.3 = (bf16[8,2,8,256]{3,0,2,1:T(8,128)(2,1)S(1)}, bf16[8,2,8,256]{3,0,2,1:T(8,128)(2,1)S(1)}, u32[]{:S(2)}, u32[]{:S(2)}) collective-permute-start(bf16[8,2,8,256]{3,0,2,1:T(8,128)(2,1)S(1)} %get-tuple-element.230), channel_id=1, source_target_pairs={{1,0},{2,1},{3,2},{5,4},{6,5},{7,6},{9,8},{10,9},{11,10},{13,12},{... | collective-permute-start | bytes 196616 | tf_op jit(solution)/shard_map/ppermute | solution.py:18
  19.8 3.4 %collective-permute-done.3 = bf16[8,2,8,256]{3,0,2,1:T(8,128)(2,1)S(1)} collective-permute-done((bf16[8,2,8,256]{3,0,2,1:T(8,128)(2,1)S(1)}, bf16[8,2,8,256]{3,0,2,1:T(8,128)(2,1)S(1)}, u32[]{:S(2)}, u32[]{:S(2)}) %collective-permute-start.3) | collective-permute-done | bytes 65568 | tf_op jit(solution)/shard_map/ppermute | solution.py:18
  23.2 0.1 constant_dynamic-update-slice_fusion.29
  23.3 0.1 constant_dynamic-update-slice_fusion.27
  23.4 0.1 constant_dynamic-update-slice_fusion.26
  23.6 0.1 constant_dynamic-update-slice_fusion.24
  23.7 0.1 constant_dynamic-update-slice_fusion.23
  23.8 0.1 constant_dynamic-update-slice_fusion.21
  23.9 0.1 constant_dynamic-update-slice_fusion.20
  24.1 0.1 constant_dynamic-update-slice_fusion.18
  24.2 0.1 constant_dynamic-update-slice_fusion.17
  24.3 0.1 constant_dynamic-update-slice_fusion.15
  24.5 0.1 constant_dynamic-update-slice_fusion.14
  24.6 0.1 constant_dynamic-update-slice_fusion.12
  24.7 0.1 constant_dynamic-update-slice_fusion.11
  24.8 0.1 constant_dynamic-update-slice_fusion.9
  25.0 0.1 constant_dynamic-update-slice_fusion.8
  25.1 0.1 constant_dynamic-update-slice_fusion.6
  25.2 0.1 constant_dynamic-update-slice_fusion.5
  25.4 0.1 constant_dynamic-update-slice_fusion.3
  25.5 0.7 multiply_convert_fusion
  28.0 0.4 fusion.24
  28.5 6.8 %all-gather.5 = f32[4,4,256]{2,1,0:T(4,128)S(1)} all-gather(f32[1,4,256]{2,1,0:T(4,128)S(1)} %bitcast.306), channel_id=4, replica_groups=mesh['groups'=2,'space'=4,'disp'=4] {'disp'}, dimensions={0}, use_global_device_ids=true | all-gather | bytes 20480 | tf_op jit(solution)/shard_map/all_gather | solution.py:26
  35.2 5.2 %all-gather.4 = f32[4,4,256]{2,1,0:T(4,128)S(1)} all-gather(f32[1,4,256]{2,1,0:T(4,128)S(1)} %bitcast.305), channel_id=3, replica_groups=mesh['groups'=2,'space'=4,'disp'=4] {'disp'}, dimensions={0}, use_global_device_ids=true | all-gather | bytes 20480 | tf_op jit(solution)/shard_map/all_gather | solution.py:26
  40.4 5.2 %all-gather.3 = f32[4,4,256]{2,1,0:T(4,128)S(1)} all-gather(f32[1,4,256]{2,1,0:T(4,128)S(1)} %bitcast.304), channel_id=2, replica_groups=mesh['groups'=2,'space'=4,'disp'=4] {'disp'}, dimensions={0}, use_global_device_ids=true | all-gather | bytes 20480 | tf_op jit(solution)/shard_map/all_gather | solution.py:26
  45.6 0.2 while.19
  46.0 3.9 %fusion.3 = f32[1,3,3,3,8,1,1]{4,0,6,5,3,2,1:T(1,128)S(1)} fusion(bf16[3,3,3,8,4,4,256]{6,3,2,1,0,5,4:T(8,128)(2,1)S(1)} %bitcast.298, bf16[4,4,256,1,1,1,1]{2,1,0,3,4,5,6:T(4,128)(2,1)S(1)} %fusion.42), kind=kOutput, calls=%fused_computation.8 | convolution fusion | flops 1769472 | bytes 1778528 | tf_op jit(solution)/shard_map/odhw,kdhw->ok/dot_general | solution.py:68
  51.6 4.5 %collective-permute-start.4 = (bf16[4,2,256]{2,1,0:T(2,128)(2,1)S(1)}, bf16[4,2,256]{2,1,0:T(2,128)(2,1)S(1)}, u32[]{:S(2)}, u32[]{:S(2)}) collective-permute-start(bf16[4,2,256]{2,1,0:T(2,128)(2,1)S(1)} %get-tuple-element.370), channel_id=1, source_target_pairs={{0,4},{4,8},{8,12},{1,5},{5,9},{9,13},{2,6},{6,10},{10,14},{3,7},{... | collective-permute-start | bytes 12296 | tf_op jit(solution)/shard_map/ppermute | solution.py:16
  56.2 1.3 %collective-permute-start.5 = (bf16[4,2,256]{2,1,0:T(2,128)(2,1)S(1)}, bf16[4,2,256]{2,1,0:T(2,128)(2,1)S(1)}, u32[]{:S(2)}, u32[]{:S(2)}) collective-permute-start(bf16[4,2,256]{2,1,0:T(2,128)(2,1)S(1)} %get-tuple-element.371), channel_id=1, source_target_pairs={{4,0},{8,4},{12,8},{5,1},{9,5},{13,9},{6,2},{10,6},{14,10},{7,3},{... | collective-permute-start | bytes 12296 | tf_op jit(solution)/shard_map/ppermute | solution.py:18
  57.5 4.2 %collective-permute-done.5 = bf16[4,2,256]{2,1,0:T(2,128)(2,1)S(1)} collective-permute-done((bf16[4,2,256]{2,1,0:T(2,128)(2,1)S(1)}, bf16[4,2,256]{2,1,0:T(2,128)(2,1)S(1)}, u32[]{:S(2)}, u32[]{:S(2)}) %collective-permute-start.5) | collective-permute-done | bytes 4128 | tf_op jit(solution)/shard_map/ppermute | solution.py:18
  61.7 1.3 %collective-permute-start.6 = (bf16[2,8,256]{2,1,0:T(8,128)(2,1)S(1)}, bf16[2,8,256]{2,1,0:T(8,128)(2,1)S(1)}, u32[]{:S(2)}, u32[]{:S(2)}) collective-permute-start(bf16[2,8,256]{2,1,0:T(8,128)(2,1)S(1)} %get-tuple-element.314), channel_id=1, source_target_pairs={{0,1},{1,2},{2,3},{4,5},{5,6},{6,7},{8,9},{9,10},{10,11},{12,13},{... | collective-permute-start | bytes 24584 | tf_op jit(solution)/shard_map/ppermute | solution.py:16
  63.0 1.3 %collective-permute-start.7 = (bf16[2,8,256]{2,1,0:T(8,128)(2,1)S(1)}, bf16[2,8,256]{2,1,0:T(8,128)(2,1)S(1)}, u32[]{:S(2)}, u32[]{:S(2)}) collective-permute-start(bf16[2,8,256]{2,1,0:T(8,128)(2,1)S(1)} %get-tuple-element.315), channel_id=1, source_target_pairs={{1,0},{2,1},{3,2},{5,4},{6,5},{7,6},{9,8},{10,9},{11,10},{13,12},{... | collective-permute-start | bytes 24584 | tf_op jit(solution)/shard_map/ppermute | solution.py:18
  64.4 3.2 %collective-permute-done.7 = bf16[2,8,256]{2,1,0:T(8,128)(2,1)S(1)} collective-permute-done((bf16[2,8,256]{2,1,0:T(8,128)(2,1)S(1)}, bf16[2,8,256]{2,1,0:T(8,128)(2,1)S(1)}, u32[]{:S(2)}, u32[]{:S(2)}) %collective-permute-start.7) | collective-permute-done | bytes 8224 | tf_op jit(solution)/shard_map/ppermute | solution.py:18
  67.7 0.6 pad_slice_fusion.93
  68.3 0.6 pad_slice_fusion.92
  68.9 0.2 fusion.32
  69.2 1.7 %concatenate.74 = bf16[27,6,6,256]{3,0,2,1:T(8,128)(2,1)S(1)} concatenate(bf16[1,6,6,256]{3,0,2,1:T(2,128)(2,1)S(1)} %get-tuple-element.257, bf16[1,6,6,256]{3,0,2,1:T(2,128)(2,1)S(1)} %get-tuple-element.256, bf16[1,6,6,256]{3,0,2,1:T(2,128)(2,1)S(1)} %get-tuple-element.232, bf16[1,6,6,256]{3,0,2,1:T(2,128)(2,1)S(1)} %get-tuple-element.233, ...), dimensions={0} | concatenate | bytes 995328 | tf_op jit(solution)/shard_map/concatenate | solution.py:37
  70.9 0.2 fusion.7
  71.1 0.1 convert_reduce_fusion
  71.4 1.0 copy-done.1
  72.4 0.6 fusion.8
  72.9 0.1 mul.133
  73.1 14.4 %all-reduce.5 = (f32[3,3,3,8,8]{4,2,1,0,3:T(4,128)S(1)}, f32[8]{0:T(128)S(1)}, f32[3,3,3,8]{3,2,1,0:T(4,128)S(1)}) all-reduce(f32[3,3,3,8,8]{4,2,1,0,3:T(4,128)S(1)} %bitcast.299, f32[8]{0:T(128)S(1)} %broadcast_multiply_fusion, f32[3,3,3,8]{3,2,1,0:T(4,128)S(1)} %bitcast_multiply_fusion.2), channel_id=1, replica_groups=mesh['groups'=2,'space'=4,'disp'=4] {'disp'}, use_global_device_ids=true, to_apply=%region_5.6 | all-reduce | flops 1952 | bytes 15616 | tf_op jit(solution)/shard_map/psum | solution.py:151
  87.5 20.9 %all-reduce.6 = (f32[3,3,3,8,8]{4,2,1,0,3:T(4,128)S(1)}, f32[8]{0:T(128)}, f32[3,3,3,8]{3,2,1,0:T(4,128)}) all-reduce(f32[3,3,3,8,8]{4,2,1,0,3:T(4,128)S(1)} %get-tuple-element.217, f32[8]{0:T(128)S(1)} %get-tuple-element.218, f32[3,3,3,8]{3,2,1,0:T(4,128)S(1)} %get-tuple-element.219), channel_id=1, replica_groups=mesh['groups'=2,'space'=4,'disp'=4] {'space'}, use_global_device_ids=true, to_apply=%region_6.7 | all-reduce | flops 1952 | bytes 15616 | tf_op jit(solution)/shard_map/psum | solution.py:150
  108.3 0.7 copy.138
  110.7 0.4 convolution_convert_fusion
  111.1 0.7 copy.137
  (171 shorter events, 8.1 us)
Async XLA Ops:
  1.5 14.5 %collective-permute-start = (bf16[8,4,2,256]{3,0,2,1:T(8,128)(2,1)S(1)}, bf16[8,4,2,256]{3,0,2,1:T(8,128)(2,1)S(1)}, u32[]{:S(2)}, u32[]{:S(2)}) collective-permute-start(bf16[8,4,2,256]{3,0,2,1:T(8,128)(2,1)S(1)} %get-tuple-element.259), channel_id=1, source_target_pairs={{0,4},{4,8},{8,12},{1,5},{5,9},{9,13},{2,6},{6,10},{10,14},{3,7},{... | collective-permute-start | bytes 98312 | tf_op jit(solution)/shard_map/ppermute | solution.py:16
  6.5 10.5 %collective-permute-start.1 = (bf16[8,4,2,256]{3,0,2,1:T(8,128)(2,1)S(1)}, bf16[8,4,2,256]{3,0,2,1:T(8,128)(2,1)S(1)}, u32[]{:S(2)}, u32[]{:S(2)}) collective-permute-start(bf16[8,4,2,256]{3,0,2,1:T(8,128)(2,1)S(1)} %get-tuple-element.258), channel_id=1, source_target_pairs={{4,0},{8,4},{12,8},{5,1},{9,5},{13,9},{6,2},{10,6},{14,10},{7,3},{... | collective-permute-start | bytes 98312 | tf_op jit(solution)/shard_map/ppermute | solution.py:18
  17.0 2.8 %collective-permute-start.2 = (bf16[8,2,8,256]{3,0,2,1:T(8,128)(2,1)S(1)}, bf16[8,2,8,256]{3,0,2,1:T(8,128)(2,1)S(1)}, u32[]{:S(2)}, u32[]{:S(2)}) collective-permute-start(bf16[8,2,8,256]{3,0,2,1:T(8,128)(2,1)S(1)} %get-tuple-element.229), channel_id=1, source_target_pairs={{0,1},{1,2},{2,3},{4,5},{5,6},{6,7},{8,9},{9,10},{10,11},{12,13},{... | collective-permute-start | bytes 196616 | tf_op jit(solution)/shard_map/ppermute | solution.py:16
  18.5 4.7 %collective-permute-start.3 = (bf16[8,2,8,256]{3,0,2,1:T(8,128)(2,1)S(1)}, bf16[8,2,8,256]{3,0,2,1:T(8,128)(2,1)S(1)}, u32[]{:S(2)}, u32[]{:S(2)}) collective-permute-start(bf16[8,2,8,256]{3,0,2,1:T(8,128)(2,1)S(1)} %get-tuple-element.230), channel_id=1, source_target_pairs={{1,0},{2,1},{3,2},{5,4},{6,5},{7,6},{9,8},{10,9},{11,10},{13,12},{... | collective-permute-start | bytes 196616 | tf_op jit(solution)/shard_map/ppermute | solution.py:18
  24.7 0.8 copy-start.6
  27.4 1.0 copy-start.4
  27.6 18.2 %copy-start.5 = (f32[4,256]{1,0:T(4,128)S(1)}, f32[4,256]{1,0:T(4,128)}, u32[]{:S(2)}) copy-start(f32[4,256]{1,0:T(4,128)} %param.13) | copy-start | bytes 12292
  45.8 4.4 %copy-start.3 = (f32[4,256]{1,0:T(4,128)}, f32[4,256]{1,0:T(4,128)S(1)}, u32[]{:S(2)}) copy-start(f32[4,256]{1,0:T(4,128)S(1)} %div.23) | copy-start | bytes 12292
  49.9 0.9 copy-start.2
  51.6 5.9 %collective-permute-start.4 = (bf16[4,2,256]{2,1,0:T(2,128)(2,1)S(1)}, bf16[4,2,256]{2,1,0:T(2,128)(2,1)S(1)}, u32[]{:S(2)}, u32[]{:S(2)}) collective-permute-start(bf16[4,2,256]{2,1,0:T(2,128)(2,1)S(1)} %get-tuple-element.370), channel_id=1, source_target_pairs={{0,4},{4,8},{8,12},{1,5},{5,9},{9,13},{2,6},{6,10},{10,14},{3,7},{... | collective-permute-start | bytes 12296 | tf_op jit(solution)/shard_map/ppermute | solution.py:16
  56.2 5.5 %collective-permute-start.5 = (bf16[4,2,256]{2,1,0:T(2,128)(2,1)S(1)}, bf16[4,2,256]{2,1,0:T(2,128)(2,1)S(1)}, u32[]{:S(2)}, u32[]{:S(2)}) collective-permute-start(bf16[4,2,256]{2,1,0:T(2,128)(2,1)S(1)} %get-tuple-element.371), channel_id=1, source_target_pairs={{4,0},{8,4},{12,8},{5,1},{9,5},{13,9},{6,2},{10,6},{14,10},{7,3},{... | collective-permute-start | bytes 12296 | tf_op jit(solution)/shard_map/ppermute | solution.py:18
  61.7 2.7 %collective-permute-start.6 = (bf16[2,8,256]{2,1,0:T(8,128)(2,1)S(1)}, bf16[2,8,256]{2,1,0:T(8,128)(2,1)S(1)}, u32[]{:S(2)}, u32[]{:S(2)}) collective-permute-start(bf16[2,8,256]{2,1,0:T(8,128)(2,1)S(1)} %get-tuple-element.314), channel_id=1, source_target_pairs={{0,1},{1,2},{2,3},{4,5},{5,6},{6,7},{8,9},{9,10},{10,11},{12,13},{... | collective-permute-start | bytes 24584 | tf_op jit(solution)/shard_map/ppermute | solution.py:16
  63.0 4.6 %collective-permute-start.7 = (bf16[2,8,256]{2,1,0:T(8,128)(2,1)S(1)}, bf16[2,8,256]{2,1,0:T(8,128)(2,1)S(1)}, u32[]{:S(2)}, u32[]{:S(2)}) collective-permute-start(bf16[2,8,256]{2,1,0:T(8,128)(2,1)S(1)} %get-tuple-element.315), channel_id=1, source_target_pairs={{1,0},{2,1},{3,2},{5,4},{6,5},{7,6},{9,8},{10,9},{11,10},{13,12},{... | collective-permute-start | bytes 24584 | tf_op jit(solution)/shard_map/ppermute | solution.py:18
  64.4 3.2 %copy-start = (bf16[216,4,4,256]{3,0,2,1:T(8,128)(2,1)}, bf16[216,4,4,256]{3,0,2,1:T(8,128)(2,1)S(1)}, u32[]{:S(2)}) copy-start(bf16[216,4,4,256]{3,0,2,1:T(8,128)(2,1)S(1)} %constant_dynamic-update-slice_fusion.84) | copy-start | bytes 5308420
  70.9 1.5 %copy-start.1 = (bf16[216,4,4,256]{3,0,2,1:T(8,128)(2,1)S(1)}, bf16[216,4,4,256]{3,0,2,1:T(8,128)(2,1)}, u32[]{:S(2)}) copy-start(bf16[216,4,4,256]{3,0,2,1:T(8,128)(2,1)} %copy-done) | copy-start | bytes 5308420
